TPU v7x, 1024 devices: a whole 4x4x32 slice. The times are simulated.
1024 devices in a mesh: rep: 4 (over z_hi), fsdp: 256 (over z_lo, y, x, core).
Axes of the slice: x: 4, y: 4, z: 32 (z_hi: 4, z_lo: 8; z = z_hi * 8 + z_lo), core: 2. Of those that a mesh axis runs over, the one named last changes fastest.
Arguments:
- hidden: bfloat16 [262144, 4096], P(('rep', 'fsdp')), may hold values from -6 to 6
- weight: bfloat16 [512, 4096], P('fsdp'), may hold values from -0.09375 to 0.09375
- adapter_a: float32 [4096, 128], P('fsdp'), may hold values from -0.09375 to 0.09375
- adapter_b: float32 [512, 128], P('fsdp'), may hold values from -0.25 to 0.25
- grad_a: float32 [4, 4096, 128], P('rep', 'fsdp'), may hold values from -0.09375 to 0.09375
- grad_b: float32 [4, 512, 128], P('rep', 'fsdp'), may hold values from -0.25 to 0.25
Outputs:
- projected: bfloat16 [262144, 512], P(('rep', 'fsdp'))
- merged: bfloat16 [512, 4096], P('fsdp')
All inputs are finite; a program needn't handle non-finite values.
Results may differ from a plain program's by a relative error of at most 0.0049.
Values may be sent and summed in bfloat16 or wider, within the bound.
A program may use at most 64 MiB of HBM per device.

v0:
```python
import jax
import jax.numpy as jnp
from jax import lax
from jax.sharding import Mesh
from jax.sharding import PartitionSpec as P

FSDP = ("fsdp_0", "fsdp_1", "fsdp_2", "fsdp_3")
REP_FSDP = ("rep", "fsdp_0", "fsdp_1", "fsdp_2", "fsdp_3")


step_size = 0.5


def in_one(arrays, axis):
    line, at, finished = (jnp.concatenate([a.reshape(-1) for a in arrays]), 0, [])
    total = lax.psum(line, axis)
    for a in arrays:
        finished.append(total[at : at + a.size].reshape(a.shape))
        at += a.size
    return tuple(finished)


def joined_along(parts, dim):
    dims = list(parts.shape[1:])
    dims[dim] *= parts.shape[0]
    return jnp.moveaxis(parts, 0, dim).reshape(dims)


def gather_in_order(shard, axes, turns):
    parts = shard
    for k in turns:
        parts = lax.all_gather(parts, axes[k])
    done = turns[::-1]
    back = [done.index(k) for k in range(len(axes))]
    parts = parts.transpose(*back, *range(len(axes), parts.ndim))
    return parts.reshape(-1, *shard.shape)


def gather_axes(shard, axes, turns, dim):
    return joined_along(gather_in_order(shard, axes, turns), dim)


def low_rank(b_rows, full_a):
    return lax.dot_general(
        b_rows,
        full_a,
        (((1,), (1,)), ((), ())),
        precision=lax.Precision.HIGHEST,
        preferred_element_type=jnp.float32,
    )


def merge_rows(rows, b_rows, full_a):
    return (rows.astype(jnp.float32) + low_rank(b_rows, full_a)).astype(jnp.bfloat16)


def shards(hidden, weight, adapter_a, adapter_b, grad_a, grad_b):
    replicas = lax.axis_size("rep")
    summed = in_one((grad_a[0], grad_b[0]), "rep")
    new_a = adapter_a - step_size * (summed[0] / replicas)
    new_b = adapter_b - step_size * (summed[1] / replicas)
    full_a = gather_axes(new_a, FSDP, (0, 1, 2, 3), 0)
    own_rows = merge_rows(weight, new_b, full_a)
    quarter = own_rows.shape[1] // replicas
    offset = lax.axis_index("rep") * quarter
    local_block = lax.dynamic_slice_in_dim(own_rows, offset, quarter, 1)[None]
    blocks = lax.all_gather(local_block, REP_FSDP, axis=0, tiled=True)
    blocks = blocks.reshape(replicas, -1, quarter)
    split_hidden = hidden.reshape(hidden.shape[0], replicas, quarter)
    output = jnp.einsum("tkc,koc->to", split_hidden, blocks, preferred_element_type=jnp.float32)
    return (output.astype(jnp.bfloat16), own_rows)


def solution(mesh):
    finer = Mesh(
        mesh.devices.reshape(mesh.shape["rep"], 8, 4, 4, 2),
        ("rep", "fsdp_0", "fsdp_1", "fsdp_2", "fsdp_3"),
    )
    in_specs = (
        P(REP_FSDP, None),
        P(FSDP, None),
        P(FSDP, None),
        P(FSDP, None),
        P("rep", FSDP, None),
        P("rep", FSDP, None),
    )
    out_specs = (P(REP_FSDP, None), P(FSDP, None))
    return jax.shard_map(
        shards, mesh=finer, in_specs=in_specs, out_specs=out_specs, check_vma=False
    )
```

profile of v0, /device:TPU:1, one launch (start us, length us, event | category | flops | bytes accessed | tf_op | source)
XLA Modules:
  0.0 593.2 jit_solution(50937377701853071)
XLA Ops:
  7.2 0.0 all-gather.10.cloned.1.call-start
  7.2 0.7 pad_maximum_fusion
  7.9 47.2 %psum.7 = f32[2304]{0:T(1024)S(1)} all-reduce(f32[2304]{0:T(1024)S(1)} %pad_maximum_fusion), channel_id=1, replica_groups=mesh['rep'=4,'fsdp_0'=8,'fsdp_1'=4,'fsdp_2'=4,'fsdp_3'=2] {'rep'}, use_global_device_ids=true, to_apply=%region_0.0 | all-reduce | flops 2304 | bytes 18432 | tf_op jit(solution)/shard_map/psum | solution.py:16
  55.2 0.7 fusion.14
  55.9 39.9 %all-gather = f32[128,128]{1,0:T(8,128)S(1)} all-gather(f32[16,128]{1,0:T(8,128)S(1)} %fusion.14), channel_id=2, replica_groups=mesh['rep'=4,'fsdp_0'=8,'fsdp_1'=4,'fsdp_2'=4,'fsdp_3'=2] {'fsdp_0'}, dimensions={0}, use_global_device_ids=true | all-gather | bytes 73728 | tf_op jit(solution)/shard_map/all_gather | solution.py:32
  95.7 10.6 %all-gather.1 = f32[32,16,128]{2,1,0:T(8,128)} all-gather(f32[8,16,128]{2,1,0:T(8,128)S(1)} %bitcast.44), channel_id=3, replica_groups=mesh['rep'=4,'fsdp_0'=8,'fsdp_1'=4,'fsdp_2'=4,'fsdp_3'=2] {'fsdp_1'}, dimensions={0}, use_global_device_ids=true | all-gather | bytes 327680 | tf_op jit(solution)/shard_map/all_gather | solution.py:32
  106.3 0.0 all-gather.10.cloned.1.call-update
  106.4 0.0 all-gather.12.cloned.1.call-start
  106.4 42.9 %all-gather.10.cloned.1.call-done = f32[16,8,16,128]{3,2,1,0:T(8,128)} async-done(((f32[4,8,16,128]{3,2,1,0:T(8,128)}), f32[16,8,16,128]{3,2,1,0:T(8,128)}) %all-gather.10.cloned.1.call-update) | async-done | bytes 1048592 | tf_op jit(solution)/shard_map/all_gather | solution.py:32
  149.3 0.0 all-gather.12.cloned.1.call-update
  149.4 0.0 all-gather.14.cloned.1.call-start
  149.4 39.4 %all-gather.12.cloned.1.call-done = f32[8,4,8,16,128]{4,3,2,1,0:T(8,128)} async-done(((f32[4,4,8,16,128]{4,3,2,1,0:T(8,128)}), f32[8,4,8,16,128]{4,3,2,1,0:T(8,128)}) %all-gather.12.cloned.1.call-update) | async-done | bytes 2097168 | tf_op jit(solution)/shard_map/all_gather | solution.py:32
  188.9 1.9 copy.15
  190.7 0.0 copy-done.1
  190.7 0.0 copy-done.2
  190.8 1.8 fusion
  192.6 0.6 dynamic-slice_bitcast_fusion
  193.2 0.0 all-gather.14.cloned.1.call-update
  193.2 0.0 copy-start.3
  193.2 381.8 %all-gather.14.cloned.1.call-done = bf16[1024,2,1024]{2,1,0:T(2,128)(2,1)} async-done(((bf16[1,2,1024]{2,1,0:T(2,128)(2,1)}), bf16[1024,2,1024]{2,1,0:T(2,128)(2,1)}) %all-gather.14.cloned.1.call-update) | async-done | bytes 4194320 | tf_op jit(solution)/shard_map/all_gather | solution.py:67
  575.0 7.3 %reshape.32 = bf16[4,512,1024]{2,1,0:T(8,128)(2,1)} reshape(bf16[1024,2,1024]{2,1,0:T(2,128)(2,1)} %all-gather.14.cloned.1.call-done) | data formatting | bytes 8388608 | tf_op jit(solution)/shard_map/reshape | solution.py:68
  582.3 0.0 copy-done
  582.3 3.5 fusion.10
  585.8 0.8 copy.17
  (4 shorter events, 0.0 us)
Async XLA Ops:
  7.2 142.2 %all-gather.10.cloned.1.call-start = ((), (), s32[]{:S(2)}) async-start(), calls=%async_computation | async-start | bytes 1310720 | tf_op jit(solution)/shard_map/all_gather | solution.py:32
  106.4 82.5 %all-gather.12.cloned.1.call-start = ((), (), s32[]{:S(2)}) async-start(), calls=%async_computation.1 | async-start | bytes 3145728 | tf_op jit(solution)/shard_map/all_gather | solution.py:32
  149.4 425.7 %all-gather.14.cloned.1.call-start = ((), (), s32[]{:S(2)}) async-start(), calls=%async_computation.2 | async-start | bytes 4198400 | tf_op jit(solution)/shard_map/all_gather | solution.py:67
  188.9 1.9 copy-start.1
  188.9 1.9 copy-start.2
  192.6 389.7 %copy-start = (bf16[2,4096]{1,0:T(2,128)(2,1)}, bf16[2,4096]{1,0:T(2,128)(2,1)S(1)}, u32[]{:S(2)}) copy-start(bf16[2,4096]{1,0:T(2,128)(2,1)S(1)} %fusion) | copy-start | bytes 49156
  193.2 389.1 %copy-start.3 = (bf16[256,4096]{1,0:T(8,128)(2,1)S(1)}, bf16[256,4096]{1,0:T(8,128)(2,1)}, u32[]{:S(2)}) copy-start(bf16[256,4096]{1,0:T(8,128)(2,1)} %param.6) | copy-start | bytes 6291460
Sparse Core Ops, SparseCore 0:
  106.5 42.8 all-gather.9
  152.0 36.7 all-gather.11
  195.2 379.7 all-gather.13
where the time goes:
time: 594 us; the launch traced here: 593 us
  waiting for transfers between devices  464 us (78%)
  blocking collectives  97.7 us (16%)
  between operations  13.8 us (2%)
  local copies, waits for them, and re-layouts  10.6 us (2%)
    all_gather x1, waiting for transfers between devices, shards(): blocks = lax.all_gather(local_block, REP_FSDP, axis=0, tiled=True)  382 us
    all_gather x2, waiting for transfers between devices, gather_in_order(): parts = lax.all_gather(parts, axes[k])  82.4 us
    all_gather x2, blocking collectives, gather_in_order(): parts = lax.all_gather(parts, axes[k])  50.5 us
    psum x1, blocking collectives, in_one(): total = lax.psum(line, axis)  47.2 us
  transfers between devices with their start and end apart: 3, of which 3 were waited for; matrix products, arithmetic and copies ran while one was open for 0% of the time, Pallas kernels for 0%

commit v1 on v0

v1 whole, which is shorter than its diff:
```python
import jax
import jax.numpy as jnp
from jax import lax
from jax.experimental import pallas as pl
from jax.experimental.pallas import tpu as pltpu
from jax.sharding import Mesh
from jax.sharding import PartitionSpec as P

FSDP = ("fsdp_0", "fsdp_1", "fsdp_2", "fsdp_3")
REP_FSDP = ("rep", "fsdp_0", "fsdp_1", "fsdp_2", "fsdp_3")
MESH = pl.DeviceIdType.MESH
bf16, f32 = jnp.bfloat16, jnp.float32
NT = (((1,), (1,)), ((), ()))
step_size = 0.5


def split(v):
    hi = v.astype(bf16)
    return hi, (v - hi.astype(f32)).astype(bf16)


def dot_nt(a, b):
    return lax.dot_general(a, b, NT, preferred_element_type=f32)


def kernel(
    hid, wt, aa, ab, ga, gb, out, mrg,
    H, W, Pb, Pin, U, Uin, A, B, Bh, Bl, aav, abv, gav, gbv, Gr, Gbr, na, nb, nbp, BL, D, Din, wv,
    s_loc, s_own, s_g, r_g, s_g2, r_g2, s_wz, r_wz, s_wf, r_w, s_ws, s_w2, r_w2,
    s_az, r_az, s_bz, r_bz, s_af, s_as, r_a, s_bf, s_bs, r_b, s_d2d, r_d2d,
):
    r, z, y, x, c = (lax.axis_index(n) for n in REP_FSDP)
    gz = r * 8 + z
    zh, zs = lax.div(z, 4), lax.rem(z, 4)
    oc = 1 - c

    def dev(dz=0, dy=0, dx=0, core=c):
        g = lax.rem(gz + (dz + 32), 32)
        return (lax.div(g, 8), lax.rem(g, 8), lax.rem(y + dy, 4), lax.rem(x + dx, 4), core)

    F = [dev(dy=k * c, dx=k * oc) for k in range(4)]
    S = [dev(dy=k * oc, dx=k * c) for k in range(4)]
    partner = dev(core=oc)
    up, down = dev(dz=8), dev(dz=-8)
    far = 4 - 8 * c
    near = [dict(dz=d) for d in (1, -1, 2, -2, 3, -3)]
    zpeers = [dev(**n) for n in near] + [dev(dz=far)]
    zpairs = [(p[:4] + (0,), p[:4] + (1,)) for p in zpeers]
    opposite = dev(dz=-far)

    def at_f(k, s=0):
        return (
            lax.rem(y + (k * c + s * oc), 4),
            lax.rem(x + (k * oc + s * c), 4),
        )

    pending = []

    def send(src, dst, ss, rs, to):
        d = pltpu.make_async_remote_copy(
            src_ref=src, dst_ref=dst, send_sem=ss, recv_sem=rs, device_id=to, device_id_type=MESH
        )
        d.start()
        pending.append(d)

    def arrive(dst, rs):
        pltpu.make_async_copy(dst, dst, rs).wait()

    mine = pl.ds(pl.multiple_of(c * 2048, 2048), 2048)
    other = pl.ds(pl.multiple_of(oc * 2048, 2048), 2048)
    rows2 = pl.ds(4 * x + 2 * c, 2)
    loads = [
        pltpu.make_async_copy(ga.at[0], gav, s_loc.at[0]),
        pltpu.make_async_copy(gb.at[0], gbv, s_loc.at[1]),
        pltpu.make_async_copy(aa, aav, s_loc.at[2]),
        pltpu.make_async_copy(ab, abv, s_loc.at[3]),
        pltpu.make_async_copy(wt, wv, s_loc.at[4]),
        pltpu.make_async_copy(hid.at[:, mine], H.at[c], s_loc.at[5]),
    ]
    for l in loads:
        l.start()
    pltpu.make_async_copy(wt.at[:, mine], W.at[z, y, rows2, :], r_wz.at[z, c]).start()

    barrier = pltpu.get_barrier_semaphore()
    peers = [partner, up, down] + F[1:] + S[1:]
    for pair in zpairs + [(opposite[:4] + (0,), opposite[:4] + (1,))]:
        peers += list(pair)
    for p in peers:
        pl.semaphore_signal(barrier, inc=1, device_id=p, device_id_type=MESH)
    pl.semaphore_wait(barrier, len(peers))

    for i, to in enumerate((up, down)):
        send(ga.at[0], Gr.at[i], s_g.at[0, i], r_g.at[0, i], to)
        send(gb.at[0], Gbr.at[i], s_g.at[1, i], r_g.at[1, i], to)
    for j, pair in enumerate(zpairs):
        for h in range(2):
            send(wt.at[:, h * 2048 : h * 2048 + 2048], W.at[z, y, rows2, :], s_wz.at[j, h], r_wz.at[z, c], pair[h])
    send(wt.at[:, other], W.at[z, y, rows2, :], s_wz.at[7, 0], r_wz.at[z, c], partner)
    send(hid.at[:, other], H.at[c], s_d2d.at[0], r_d2d.at[0], partner)

    def wslab(yy, xx):
        return W.at[:, yy, pl.ds(4 * xx, 4), :]

    def whalf(yy, xx, h):
        return W.at[pl.ds(4 * h, 4), yy, pl.ds(4 * xx, 4), :]

    for zz in range(8):
        for cs in range(2):
            arrive(W.at[zz, y, pl.ds(4 * x + 2 * cs, 2), :], r_wz.at[zz, cs])
    for k in (1, 3, 2):
        send(wslab(y, x), wslab(y, x), s_wf.at[k - 1], r_w.at[y, x], F[k])

    for i in range(2):
        arrive(Gr.at[i], r_g.at[0, i])
        arrive(Gbr.at[i], r_g.at[1, i])
    send(Gr.at[0, 0:8], Gr.at[2, 0:8], s_g2.at[0], r_g2.at[0], up)
    send(Gr.at[1, 8:16], Gr.at[2, 8:16], s_g2.at[1], r_g2.at[1], down)
    send(Gbr.at[0], Gbr.at[2], s_g2.at[2], r_g2.at[2], up)

    for k in range(4):
        yy, xx = at_f(k)
        if k:
            arrive(wslab(yy, xx), r_w.at[yy, xx])
        for i, s in enumerate((1, 3)):
            send(wslab(yy, xx), wslab(yy, xx), s_ws.at[k, i], r_w.at[yy, xx], S[s])

    for l in loads[:5]:
        l.wait()
    arrive(Gr.at[2, 0:8], r_g2.at[0])
    arrive(Gr.at[2, 8:16], r_g2.at[1])
    arrive(Gbr.at[2], r_g2.at[2])
    scale = step_size / 4
    na[...] = (aav[...] - scale * ((gav[...] + Gr[0]) + (Gr[1] + Gr[2]))).astype(bf16)
    newb = abv[...] - scale * ((gbv[...] + Gbr[0]) + (Gbr[1] + Gbr[2]))
    nb[...] = newb
    adst = A.at[zs, y, x, pl.ds(16 * c, 16), :]
    bdst = B.at[z, y, x, pl.ds(2 * c, 2), :]
    for j, p in enumerate(zpeers):
        to = p[:4] + (zh,)
        send(na, adst, s_az.at[j], r_az.at[zs, c], to)
        send(nb, bdst, s_bz.at[j], r_bz.at[zs, c], to)
    own_a = pltpu.make_async_copy(na, adst, r_az.at[zs, c])
    own_b = pltpu.make_async_copy(nb, bdst, r_bz.at[zs, c])
    give_a = pltpu.make_async_remote_copy(na, adst, s_own.at[0], r_az.at[zs, c], partner, MESH)
    give_b = pltpu.make_async_remote_copy(nb, bdst, s_own.at[1], r_bz.at[zs, c], partner, MESH)

    @pl.when(zh == c)
    def _():
        own_a.start()
        own_b.start()

    @pl.when(zh != c)
    def _():
        give_a.start()
        give_b.start()

    send(nb, nbp, s_d2d.at[1], r_d2d.at[1], partner)

    fabs = x * oc + y * c
    for k in range(4):
        for i, (s, to) in enumerate(((3, 1), (1, 3))):
            yy, xx = at_f(k, s)
            arrive(wslab(yy, xx), r_w.at[yy, xx])
            send(whalf(yy, xx, i), whalf(yy, xx, i), s_w2.at[k, i], r_w2.at[lax.rem(fabs + k, 4), i], S[to])

    bz = pl.ds(4 * c, 4)
    for q in range(4):
        for cs in range(2):
            arrive(A.at[q, y, x, pl.ds(16 * cs, 16), :], r_az.at[q, cs])
            arrive(B.at[4 * c + q, y, x, pl.ds(2 * cs, 2), :], r_bz.at[q, cs])
    for k in (1, 3, 2):
        send(A.at[:, y, x], A.at[:, y, x], s_af.at[k - 1], r_a.at[y, x], F[k])
        send(B.at[bz, y, x], B.at[bz, y, x], s_bf.at[k - 1], r_b.at[y, x], F[k])
    for k in (0, 1, 3, 2):
        yy, xx = at_f(k)
        if k:
            arrive(A.at[:, yy, xx], r_a.at[yy, xx])
            arrive(B.at[bz, yy, xx], r_b.at[yy, xx])
        for s in (1, 3, 2):
            send(A.at[:, yy, xx], A.at[:, yy, xx], s_as.at[k, s - 1], r_a.at[yy, xx], S[s])
            send(B.at[bz, yy, xx], B.at[bz, yy, xx], s_bs.at[k, s - 1], r_b.at[yy, xx], S[s])

    for k in range(4):
        for i in range(2):
            yy, xx = at_f(k, 2)
            arrive(whalf(yy, xx, i), r_w2.at[lax.rem(fabs + k, 4), i])
    arrive(H.at[oc], r_d2d.at[0])
    loads[5].wait()

    def project(t):
        def tile(n, carry):
            w = W[pl.ds(4 * n, 4)].reshape(256, 2048)
            Pb[t, :, pl.ds(pl.multiple_of(n * 256, 256), 256)] = dot_nt(H[t], w)
            return carry

        lax.fori_loop(0, 2, tile, 0)

    project(oc)
    send(Pb.at[oc], Pin, s_d2d.at[2], r_d2d.at[2], partner)
    project(c)

    for k in range(4):
        for s in (1, 3, 2):
            yy, xx = at_f(k, s)
            arrive(B.at[bz, yy, xx], r_b.at[yy, xx])
    send(B.at[bz], B.at[bz], s_d2d.at[3], r_d2d.at[3], partner)
    for k in range(4):
        for s in (1, 3, 2):
            yy, xx = at_f(k, s)
            arrive(A.at[:, yy, xx], r_a.at[yy, xx])
    full_a = A[...].reshape(2048, 128)
    U[oc] = jnp.dot(H[oc], full_a, preferred_element_type=f32)
    send(U.at[oc], Uin, s_d2d.at[4], r_d2d.at[4], partner)

    arrive(nbp, r_d2d.at[1])
    hi, lo = split(newb)
    BL[0:2, :] = hi.astype(f32)
    BL[4:6, :] = lo.astype(f32)
    hi, lo = split(nbp[...])
    BL[2:4, :] = hi.astype(f32)
    BL[6:8, :] = lo.astype(f32)
    delta = dot_nt(BL[...].astype(bf16), full_a)
    D[...] = delta[2:4, :] + delta[6:8, :]
    send(D, Din, s_d2d.at[5], r_d2d.at[5], partner)
    mrg[:, mine] = (wv[:, mine].astype(f32) + (delta[0:2, :] + delta[4:6, :])).astype(bf16)

    U[c] = jnp.dot(H[c], full_a, preferred_element_type=f32)
    arrive(B.at[pl.ds(4 * oc, 4)], r_d2d.at[3])
    hi, lo = split(B.reshape(512, 128)[...])
    Bh[...] = hi
    Bl[...] = lo
    arrive(Pin, r_d2d.at[2])
    arrive(Uin, r_d2d.at[4])
    uh, ul = split(U[c] + Uin[...])
    acc = Pb[c] + Pin[...]
    acc = acc + (dot_nt(uh, Bh[...]) + (dot_nt(uh, Bl[...]) + dot_nt(ul, Bh[...])))
    out[...] = acc.astype(bf16)
    arrive(Din, r_d2d.at[5])
    mrg[:, other] = (wv[:, other].astype(f32) + Din[...]).astype(bf16)

    for d in pending:
        d.wait_send()

    @pl.when(zh != c)
    def _():
        give_a.wait_send()
        give_b.wait_send()


def shards(hidden, weight, adapter_a, adapter_b, grad_a, grad_b):
    V, sem = pltpu.VMEM, pltpu.SemaphoreType.DMA
    scratch = [
        V((2, 256, 2048), bf16),
        V((8, 4, 16, 2048), bf16),
        V((2, 256, 512), f32),
        V((256, 512), f32),
        V((2, 256, 128), f32),
        V((256, 128), f32),
        V((4, 4, 4, 32, 128), bf16),
        V((8, 4, 4, 4, 128), f32),
        V((512, 128), bf16),
        V((512, 128), bf16),
        V((16, 128), f32),
        V((2, 128), f32),
        V((16, 128), f32),
        V((2, 128), f32),
        V((3, 16, 128), f32),
        V((3, 2, 128), f32),
        V((16, 128), bf16),
        V((2, 128), f32),
        V((2, 128), f32),
        V((8, 128), f32),
        V((2, 2048), f32),
        V((2, 2048), f32),
        V((2, 4096), bf16),
        sem((6,)), sem((2,)), sem((2, 2)), sem((2, 2)), sem((3,)), sem((3,)),
        sem((8, 2)), sem((8, 2)), sem((3,)), sem((4, 4)), sem((4, 2)), sem((4, 2)), sem((4, 2)),
        sem((7,)), sem((4, 2)), sem((7,)), sem((4, 2)),
        sem((3,)), sem((4, 3)), sem((4, 4)), sem((3,)), sem((4, 3)), sem((4, 4)),
        sem((6,)), sem((6,)),
    ]
    hbm = pl.BlockSpec(memory_space=pltpu.HBM)
    vmem = pl.BlockSpec(memory_space=pltpu.VMEM)
    return pl.pallas_call(
        kernel,
        out_shape=(
            jax.ShapeDtypeStruct((256, 512), bf16),
            jax.ShapeDtypeStruct((2, 4096), bf16),
        ),
        in_specs=[hbm] * 6,
        out_specs=(vmem, vmem),
        scratch_shapes=scratch,
        compiler_params=pltpu.CompilerParams(
            collective_id=0, has_side_effects=True, vmem_limit_bytes=40 * 2**20
        ),
    )(*(pltpu.with_memory_space_constraint(a, pltpu.HBM) for a in (hidden, weight, adapter_a, adapter_b, grad_a, grad_b)))


def solution(mesh):
    finer = Mesh(
        mesh.devices.reshape(mesh.shape["rep"], 8, 4, 4, 2),
        ("rep", "fsdp_0", "fsdp_1", "fsdp_2", "fsdp_3"),
    )
    in_specs = (
        P(REP_FSDP, None),
        P(FSDP, None),
        P(FSDP, None),
        P(FSDP, None),
        P("rep", FSDP, None),
        P("rep", FSDP, None),
    )
    out_specs = (P(REP_FSDP, None), P(FSDP, None))
    return jax.shard_map(
        shards, mesh=finer, in_specs=in_specs, out_specs=out_specs, check_vma=False
    )
```

time: 594 us -> 61.6 us (0.10)
  waiting for transfers between devices: 464 us -> 0 us
  blocking collectives: 97.7 us -> 0 us
  Pallas kernels: 0 us -> 59.6 us
  between operations: 13.8 us -> 0.64 us
  local copies, waits for them, and re-layouts: 10.6 us -> 1.31 us
    all_gather x3 -> x0, waiting for transfers between devices: 464 us -> none  [the longest x1 382 us: shards(): blocks = lax.all_gather(local_block, REP_FSDP, axis=0, tiled=True)]
    pallas_call x0 -> x1, Pallas kernels: none -> 59.6 us  [shards(): pl.pallas_call(kernel, out_shape=(jax.ShapeDtypeStruct((256, 512), bf16),...]
    all_gather x2 -> x0, blocking collectives: 50.5 us -> none  [gather_in_order(): parts = lax.all_gather(parts, axes[k])]
    psum x1 -> x0, blocking collectives: 47.2 us -> none  [in_one(): total = lax.psum(line, axis)]
    reshape x1 -> x0, local copies, waits for them, and re-layouts: 7.28 us -> none  [shards(): blocks = blocks.reshape(replicas, -1, quarter)]
  transfers between devices with their start and end apart: 3 -> 0, of which waited for: 3 -> 0; matrix products, arithmetic and copies ran while one was open for 0% -> 0% of each run, Pallas kernels for 0% -> 0%
where the time goes in v1:
time: 61.6 us; the launch traced here: 61.5 us
  Pallas kernels  59.6 us (97%)
  local copies, waits for them, and re-layouts  1.31 us (2%)
  between operations  0.64 us (1%)
    pallas_call x1, Pallas kernels, shards(): pl.pallas_call(kernel, out_shape=(jax.ShapeDtypeStruct((256, 512), bf16),...  59.6 us
    unnamed x2, local copies, waits for them, and re-layouts  1.31 us

profile of v1, /device:TPU:1, one launch (start us, length us, event | category | flops | bytes accessed | tf_op | source)
XLA Modules:
  0.0 61.5 jit_solution(2322245837170794644)
XLA Ops:
  0.6 59.6 %shard_map.77 = (bf16[256,512]{1,0:T(8,128)(2,1)S(1)}, bf16[2,4096]{1,0:T(2,128)(2,1)S(1)}) custom-call(bf16[256,4096]{1,0:T(8,128)(2,1)} %hid.1, bf16[2,4096]{1,0:T(2,128)(2,1)} %wt.1, f32[16,128]{1,0:T(8,128)} %aa.1, f32[2,128]{1,0:T(2,128)} %ab.1, f32[1,16,128]{2,1,0:T(8,128)} %ga.1, f32[1,2,128]{2,1,0:T(2,128)} %gb.1), custom_call_target="tpu_custom_call" | custom-call | tf_op jit(solution)/shard_map/pallas_call | solution.py:284
  60.2 0.7 %copy.10 = bf16[256,512]{1,0:T(8,128)(2,1)} copy(bf16[256,512]{1,0:T(8,128)(2,1)S(1)} %get-tuple-element.4) | data formatting | bytes 524288
  60.9 0.6 copy.11
